TPU v7x, 512 devices: a whole 4x8x8 slice. The times are simulated.
512 devices in a mesh: lat: 16 (over y_lo, x, core), lon: 32 (over y_hi, z).
Axes of the slice: x: 4, y: 8 (y_hi: 4, y_lo: 2; y = y_hi * 2 + y_lo), z: 8, core: 2. Of those that a mesh axis runs over, the one named last changes fastest.
Arguments:
- state_block: float32 [64, 1440, 256], P('lat', 'lon'), may hold values from -5 to 5
- stored_fields: bfloat16 [64, 1440, 1024], P('lat', 'lon'), may hold values from -14 to 14
- slope_fields: bfloat16 [64, 1440, 192], P('lat', 'lon'), may hold values from 0.5 to 1.5
- kernels: bfloat16 [3, 9, 64, 64], replicated, may hold values from -0.25 to 0.25
- spectral_gains: float32 [64, 721], replicated, may hold values from 0.25 to 4
Outputs:
- next_block: float32 [64, 1440, 256], P('lat', 'lon')
- diag_coef: float32 [4, 4], replicated
- stored_coef: float32 [16, 4], replicated
- norm_factor: float32 [4, 4], replicated
All inputs are finite; a program needn't handle non-finite values.
Results may differ from a plain program's by a relative error of at most 0.0062.
Values may be sent and summed in bfloat16 or wider, within the bound.
No kernel may reach another device: no remote copies, remote signals or barrier semaphores. Data moves between devices by JAX's collectives and lax.ppermute only.
A program may use at most 64 MiB of HBM per device.

v0:
```python
import jax
import jax.numpy as jnp
from jax import lax
from jax.sharding import PartitionSpec as P

highest = lax.Precision.HIGHEST
triple = lax.Precision.HIGH


def with_halo(cells, sides, width, closed):
    for axis, dim in sides:
        count = lax.axis_size(axis)
        ends = count if closed else count - 1
        head = lax.slice_in_dim(cells, 0, width, axis=dim)
        tail = lax.slice_in_dim(cells, cells.shape[dim] - width, cells.shape[dim], axis=dim)
        cells = jnp.concatenate(
            [
                lax.ppermute(tail, axis, [(i, (i + 1) % count) for i in range(ends)]),
                cells,
                lax.ppermute(head, axis, [((i + 1) % count, i) for i in range(ends)]),
            ],
            axis=dim,
        )
    return cells


def upper_factor(gram_matrix):
    count = gram_matrix.shape[0]
    nothing = gram_matrix[0, 0] * 0.0
    entries = [[nothing for col in range(count)] for row in range(count)]
    for row in range(count):
        total = gram_matrix[row, row]
        for inner in range(row):
            total = total - entries[inner][row] * entries[inner][row]
        entries[row][row] = jnp.sqrt(total)
        for col in range(row + 1, count):
            value = gram_matrix[row, col]
            for inner in range(row):
                value = value - entries[inner][row] * entries[inner][col]
            entries[row][col] = value / entries[row][row]
    inverse = [[nothing for col in range(count)] for row in range(count)]
    for col in range(count):
        inverse[col][col] = 1.0 / entries[col][col]
        for row in range(col - 1, -1, -1):
            value = nothing
            for inner in range(row + 1, col + 1):
                value = value + entries[row][inner] * inverse[inner][col]
            inverse[row][col] = -value / entries[row][row]
    factor = jnp.stack([jnp.stack(line) for line in entries])
    inverted = jnp.stack([jnp.stack(line) for line in inverse])
    return (factor, inverted)


def widen_layer(field):
    wrapped = with_halo(field, (("lon", 1),), 1, True)
    return with_halo(wrapped, (("lat", 0),), 1, False)


def stencil(extended, matrix, out_rows, out_cols, adjoint):
    channels = matrix.shape[1]
    split = extended.reshape(extended.shape[0], extended.shape[1], -1, channels)
    pieces = []
    for row_step in range(3):
        for col_step in range(3):
            if adjoint:
                pieces.append(
                    split[
                        2 - row_step : 2 - row_step + out_rows,
                        2 - col_step : 2 - col_step + out_cols,
                    ]
                )
            else:
                pieces.append(split[row_step : row_step + out_rows, col_step : col_step + out_cols])
    stacked = jnp.concatenate(pieces, axis=3)
    return jnp.einsum("abvk,kd->abvd", stacked, matrix, preferred_element_type=jnp.float32)


def scaled(slope, values):
    product = slope.astype(jnp.float32)[:, :, None, :] * values
    return product.astype(jnp.bfloat16).reshape(values.shape[0], values.shape[1], -1)


def as_split(field, channels):
    return field.reshape(field.shape[0], field.shape[1], -1, channels).astype(jnp.float32)


def spectral(hidden, spectral_gains, channels):
    band_rows = hidden.shape[0]
    columns = lax.all_to_all(hidden, "lon", split_axis=2, concat_axis=1, tiled=True)
    full_lon = columns.shape[1]
    own_columns = columns.shape[2]
    frequency_count = spectral_gains.shape[1]
    lat_total = band_rows * lax.axis_size("lat")
    row_index = lax.axis_index("lat") * band_rows + jnp.arange(band_rows, dtype=jnp.int32)
    latitude = (row_index.astype(jnp.float32) + 0.5) / lat_total
    area_weight = jnp.cos(jnp.pi * (latitude - 0.5))
    weighted = columns.astype(jnp.float32) * area_weight[:, None, None]
    row_major = jnp.transpose(weighted, (0, 2, 1)).reshape(band_rows * own_columns, full_lon)
    points = jnp.arange(full_lon, dtype=jnp.int32)
    wave_index = jnp.arange(frequency_count, dtype=jnp.int32)
    phase_index = points[:, None] * wave_index[None, :] % full_lon
    angles = phase_index.astype(jnp.float32) * (2.0 * jnp.pi / full_lon)
    cosine = jnp.cos(angles)
    sine_table = jnp.sin(angles)
    forward_table = jnp.concatenate([cosine, -sine_table], axis=1)
    backward_table = jnp.concatenate([cosine.T, -sine_table.T], axis=0)
    spectrum = jnp.dot(row_major, forward_table, precision=triple)
    lead_channel = lax.axis_index("lon") * own_columns % channels
    chosen = lax.dynamic_slice(spectral_gains, (lead_channel, 0), (own_columns, frequency_count))
    edge_wave = (wave_index == 0) | (wave_index == full_lon // 2)
    wave_weight = jnp.where(edge_wave, 1.0 / full_lon, 2.0 / full_lon).astype(jnp.float32)
    factor = chosen * wave_weight[None, :]
    factor = jnp.concatenate([factor, factor], axis=1)
    factor_rows = jnp.broadcast_to(factor[None], (band_rows, own_columns, 2 * frequency_count))
    factor_rows = factor_rows.reshape(band_rows * own_columns, 2 * frequency_count)
    restored = jnp.dot(spectrum * factor_rows, backward_table, precision=triple)
    restored = restored.reshape(band_rows, own_columns, full_lon) * area_weight[:, None, None]
    restored = jnp.transpose(restored, (0, 2, 1)).astype(jnp.bfloat16)
    return lax.all_to_all(restored, "lon", split_axis=1, concat_axis=2, tiled=True)


def per_device(state_block, stored_fields, slope_fields, kernels, spectral_gains):
    band_rows, tile_cols, block_width = state_block.shape
    layers = kernels.shape[0]
    channels = kernels.shape[2]
    vectors = block_width // channels
    forward_mats = [kernels[layer].reshape(9 * channels, channels) for layer in range(layers)]
    adjoint_mats = [
        jnp.transpose(kernels[layer], (0, 2, 1)).reshape(9 * channels, channels)
        for layer in range(layers)
    ]
    hidden = state_block.astype(jnp.bfloat16)
    for layer in range(layers):
        extended = widen_layer(hidden)
        summed = stencil(extended, forward_mats[layer], band_rows, tile_cols, False)
        hidden = scaled(slope_fields[:, :, layer * channels : (layer + 1) * channels], summed)
    filtered = spectral(hidden, spectral_gains, channels)
    top_slope = slope_fields[:, :, (layers - 1) * channels : layers * channels]
    adjoint = scaled(top_slope, as_split(filtered, channels))
    for layer in range(layers - 1, 0, -1):
        extended = widen_layer(adjoint)
        summed = stencil(extended, adjoint_mats[layer], band_rows, tile_cols, True)
        adjoint = scaled(slope_fields[:, :, (layer - 1) * channels : layer * channels], summed)
    extended = widen_layer(adjoint)
    image = stencil(extended, adjoint_mats[0], band_rows, tile_cols, True)
    cells = band_rows * tile_cols
    weighting = 1.0 / (
        band_rows * lax.axis_size("lat") * tile_cols * lax.axis_size("lon") * channels
    )
    current = state_block.reshape(cells, vectors, channels)
    stored = stored_fields.reshape(cells, -1, channels).astype(jnp.float32)
    image_cells = image.reshape(cells, vectors, channels)
    part_diag = jnp.einsum("xvc,xwc->vw", current, image_cells, precision=highest) * weighting
    part_stored = jnp.einsum("xsc,xwc->sw", stored, image_cells, precision=highest) * weighting
    diag_coef, stored_coef = lax.psum((part_diag, part_stored), ("lat", "lon"))
    residual = image_cells - jnp.einsum("xvc,vw->xwc", current, diag_coef, precision=highest)
    residual = residual - jnp.einsum("xsc,sw->xwc", stored, stored_coef, precision=highest)
    part_gram = jnp.einsum("xvc,xwc->vw", residual, residual, precision=highest) * weighting
    gram_matrix = lax.psum(part_gram, ("lat", "lon"))
    norm_factor, inverse = upper_factor(gram_matrix)
    next_fields = jnp.einsum("xvc,vw->xwc", residual, inverse, precision=highest)
    return (
        next_fields.reshape(band_rows, tile_cols, block_width),
        diag_coef,
        stored_coef,
        norm_factor,
    )


def solution(mesh):
    return jax.shard_map(
        per_device,
        mesh=mesh,
        in_specs=(P("lat", "lon", None), P("lat", "lon", None), P("lat", "lon", None), P(), P()),
        out_specs=(P("lat", "lon", None), P(), P(), P()),
        check_vma=False,
    )
```

profile of v0, /device:TPU:1, one launch (start us, length us, event | category | flops | bytes accessed | tf_op | source)
XLA Modules:
  0.0 468.9 jit_solution(3852663739283305581)
XLA Ops:
  1.6 5.0 %collective-permute-start = (bf16[4,1,256]{2,0,1:T(4,128)(2,1)S(1)}, bf16[4,1,256]{2,0,1:T(4,128)(2,1)S(1)}, u32[]{:S(2)}, u32[]{:S(2)}) collective-permute-start(bf16[4,1,256]{2,0,1:T(4,128)(2,1)S(1)} %get-tuple-element.115), channel_id=1, source_target_pairs={{0,1},{1,2},{2,3},{3,4},{4,5},{5,6},{6,7},{7,8},{8,9},{9,10},{10,1... | collective-permute-start | bytes 6152 | tf_op jit(solution)/shard_map/ppermute | solution.py:18
  6.6 12.4 %collective-permute-start.1 = (bf16[4,1,256]{2,0,1:T(4,128)(2,1)S(1)}, bf16[4,1,256]{2,0,1:T(4,128)(2,1)S(1)}, u32[]{:S(2)}, u32[]{:S(2)}) collective-permute-start(bf16[4,1,256]{2,0,1:T(4,128)(2,1)S(1)} %get-tuple-element.116), channel_id=1, source_target_pairs={{1,0},{2,1},{3,2},{4,3},{5,4},{6,5},{7,6},{8,7},{9,8},{10,9},{11,1... | collective-permute-start | bytes 6152 | tf_op jit(solution)/shard_map/ppermute | solution.py:20
  19.0 19.7 %sine_negate_fusion.1 = (f32[1440,721]{1,0:T(8,128)}, f32[1440,721]{1,0:T(8,128)}) fusion(), kind=kLoop, calls=%fused_computation.20 | loop fusion | flops 10382400 | bytes 8305920 | tf_op jit(solution)/shard_map/neg | solution.py:105
  39.8 4.0 collective-permute-start.2
  45.8 3.3 collective-permute-done.3
  54.8 19.8 %sine_negate_fusion = (f32[721,1440]{1,0:T(8,128)}, f32[721,1440]{1,0:T(8,128)}) fusion(), kind=kLoop, calls=%fused_computation.12 | loop fusion | flops 10382400 | bytes 8305920 | tf_op jit(solution)/shard_map/neg | solution.py:106
  74.5 7.6 %collective-permute-start.5 = (bf16[4,1,256]{2,0,1:T(4,128)(2,1)S(1)}, bf16[4,1,256]{2,0,1:T(4,128)(2,1)S(1)}, u32[]{:S(2)}, u32[]{:S(2)}) collective-permute-start(bf16[4,1,256]{2,0,1:T(4,128)(2,1)S(1)} %get-tuple-element.113), channel_id=1, source_target_pairs={{1,0},{2,1},{3,2},{4,3},{5,4},{6,5},{7,6},{8,7},{9,8},{10,9},{11,1... | collective-permute-start | bytes 6152 | tf_op jit(solution)/shard_map/ppermute | solution.py:20
  82.9 3.0 collective-permute-start.6
  87.9 3.4 collective-permute-done.7
  97.7 8.1 %collective-permute-start.9 = (bf16[4,1,256]{2,0,1:T(4,128)(2,1)S(1)}, bf16[4,1,256]{2,0,1:T(4,128)(2,1)S(1)}, u32[]{:S(2)}, u32[]{:S(2)}) collective-permute-start(bf16[4,1,256]{2,0,1:T(4,128)(2,1)S(1)} %get-tuple-element.108), channel_id=1, source_target_pairs={{1,0},{2,1},{3,2},{4,3},{5,4},{6,5},{7,6},{8,7},{9,8},{10,9},{11,1... | collective-permute-start | bytes 6152 | tf_op jit(solution)/shard_map/ppermute | solution.py:20
  106.6 2.7 collective-permute-start.10
  111.4 3.4 collective-permute-done.11
  119.4 8.3 %all-to-all-start = ((bf16[32,2,720]{2,1,0:T(2,128)(2,1)}), bf16[32,2,720]{2,1,0:T(2,128)(2,1)S(1)}, u32[]{:S(2)}, u32[]{:S(2)}) async-start(bf16[32,2,720]{2,1,0:T(2,128)(2,1)} %reshape.151), calls=%async_computation | async-start | bytes 196608 | tf_op jit(solution)/shard_map/all_to_all | solution.py:89
  127.8 11.2 %all-to-all-done = bf16[32,2,720]{2,1,0:T(2,128)(2,1)S(1)} async-done(((bf16[32,2,720]{2,1,0:T(2,128)(2,1)}), bf16[32,2,720]{2,1,0:T(2,128)(2,1)S(1)}, u32[]{:S(2)}, u32[]{:S(2)}) %all-to-all-start) | async-done | bytes 92192 | tf_op jit(solution)/shard_map/all_to_all | solution.py:89
  140.0 7.0 %fusion.20 = f32[32,1442]{1,0:T(8,128)S(1)} fusion(f32[1440,721]{1,0:T(8,128)} %get-tuple-element.127, f32[1440,721]{1,0:T(8,128)} %get-tuple-element.128, f32[4,1440,8]{1,2,0:T(8,128)S(1)} %reshape.130, f32[8,1442]{1,0:T(8,128)S(1)} %pad_maximum_fusion.8, f32[4]{0:T(128)S(1)} %multiply_cosine_fusion), kind=kOutput, calls=%fused_computation.26 | convolution fusion | flops 400852864 | bytes 8720976 | tf_op jit(solution)/shard_map/dot_general | solution.py:107
  147.0 5.2 %fusion.32 = bf16[4,1440,8]{1,2,0:T(8,128)(2,1)S(1)} fusion(f32[32,1442]{1,0:T(8,128)S(1)} %fusion.20, f32[721,1440]{1,0:T(8,128)S(1)} %bitcast.190, f32[721,1440]{1,0:T(8,128)} %get-tuple-element.130, f32[4]{0:T(128)S(1)} %multiply_cosine_fusion), kind=kOutput, calls=%fused_computation.30 | convolution fusion | flops 400852800 | bytes 8582672 | tf_op jit(solution)/shard_map/dot_general | solution.py:116
  153.9 1.9 reshape.153
  155.8 3.8 all-to-all-start.1
  160.0 11.6 %all-to-all-done.1 = bf16[32,2,720]{2,1,0:T(2,128)(2,1)S(1)} async-done(((bf16[32,2,720]{2,1,0:T(2,128)(2,1)}), bf16[32,2,720]{2,1,0:T(2,128)(2,1)S(1)}, u32[]{:S(2)}, u32[]{:S(2)}) %all-to-all-start.1) | async-done | bytes 92192 | tf_op jit(solution)/shard_map/all_to_all | solution.py:119
  176.1 2.7 collective-permute-start.12
  178.8 6.8 %collective-permute-start.13 = (bf16[4,1,256]{2,0,1:T(4,128)(2,1)S(1)}, bf16[4,1,256]{2,0,1:T(4,128)(2,1)S(1)}, u32[]{:S(2)}, u32[]{:S(2)}) collective-permute-start(bf16[4,1,256]{2,0,1:T(4,128)(2,1)S(1)} %get-tuple-element.107), channel_id=1, source_target_pairs={{1,0},{2,1},{3,2},{4,3},{5,4},{6,5},{7,6},{8,7},{9,8},{10,9},{11,1... | collective-permute-start | bytes 6152 | tf_op jit(solution)/shard_map/ppermute | solution.py:20
  186.5 5.5 %collective-permute-start.14 = (bf16[1,47,256]{2,0,1:T(2,128)(2,1)S(1)}, bf16[1,47,256]{2,0,1:T(2,128)(2,1)S(1)}, u32[]{:S(2)}, u32[]{:S(2)}) collective-permute-start(bf16[1,47,256]{2,0,1:T(2,128)(2,1)S(1)} %get-tuple-element.94), channel_id=1, source_target_pairs={{0,32},{32,64},{64,96},{96,128},{128,160},{160,192},{192,224},{224... | collective-permute-start | bytes 72200 | tf_op jit(solution)/shard_map/ppermute | solution.py:18
  192.0 2.1 collective-permute-start.15
  194.9 2.5 collective-permute-done.15
  203.0 8.1 %collective-permute-start.17 = (bf16[4,1,256]{2,0,1:T(4,128)(2,1)S(1)}, bf16[4,1,256]{2,0,1:T(4,128)(2,1)S(1)}, u32[]{:S(2)}, u32[]{:S(2)}) collective-permute-start(bf16[4,1,256]{2,0,1:T(4,128)(2,1)S(1)} %get-tuple-element.104), channel_id=1, source_target_pairs={{1,0},{2,1},{3,2},{4,3},{5,4},{6,5},{7,6},{8,7},{9,8},{10,9},{11,1... | collective-permute-start | bytes 6152 | tf_op jit(solution)/shard_map/ppermute | solution.py:20
  212.0 2.7 collective-permute-start.18
  217.4 2.7 collective-permute-done.19
  224.9 8.1 %collective-permute-start.21 = (bf16[4,1,256]{2,0,1:T(4,128)(2,1)S(1)}, bf16[4,1,256]{2,0,1:T(4,128)(2,1)S(1)}, u32[]{:S(2)}, u32[]{:S(2)}) collective-permute-start(bf16[4,1,256]{2,0,1:T(4,128)(2,1)S(1)} %get-tuple-element.102), channel_id=1, source_target_pairs={{1,0},{2,1},{3,2},{4,3},{5,4},{6,5},{7,6},{8,7},{9,8},{10,9},{11,1... | collective-permute-start | bytes 6152 | tf_op jit(solution)/shard_map/ppermute | solution.py:20
  233.8 2.7 collective-permute-start.22
  243.9 3.3 concatenate.83
  250.7 108.5 %all-reduce = (f32[16,4]{0,1:T(4,128)S(1)}, f32[4,4]{0,1:T(4,128)S(1)}) all-reduce(f32[16,4]{0,1:T(4,128)S(1)} %fusion.43, f32[4,4]{0,1:T(4,128)S(1)} %fusion.44), channel_id=1, replica_groups=mesh['lat'=16,'lon'=32] {'lat','lon'}, use_global_device_ids=true, to_apply=%region_1.2 | all-reduce | flops 80 | bytes 640 | tf_op jit(solution)/shard_map/psum | solution.py:155
  361.5 94.6 %psum.23 = f32[4,4]{1,0:T(4,128)S(1)} all-reduce(f32[4,4]{1,0:T(4,128)S(1)} %fusion.41), channel_id=1, replica_groups=mesh['lat'=16,'lon'=32] {'lat','lon'}, use_global_device_ids=true, to_apply=%region_2.3 | all-reduce | flops 16 | bytes 128 | tf_op jit(solution)/shard_map/psum | solution.py:159
  (213 shorter events, 67.0 us)
Async XLA Ops:
  1.6 37.1 %copy-start.3 = (bf16[3,9,64,64]{3,2,1,0:T(8,128)(2,1)S(1)}, bf16[3,9,64,64]{3,2,1,0:T(8,128)(2,1)}, u32[]{:S(2)}) copy-start(bf16[3,9,64,64]{3,2,1,0:T(8,128)(2,1)} %param.8) | copy-start | bytes 663556
  1.6 38.0 %collective-permute-start = (bf16[4,1,256]{2,0,1:T(4,128)(2,1)S(1)}, bf16[4,1,256]{2,0,1:T(4,128)(2,1)S(1)}, u32[]{:S(2)}, u32[]{:S(2)}) collective-permute-start(bf16[4,1,256]{2,0,1:T(4,128)(2,1)S(1)} %get-tuple-element.115), channel_id=1, source_target_pairs={{0,1},{1,2},{2,3},{3,4},{4,5},{5,6},{6,7},{7,8},{8,9},{9,10},{10,1... | collective-permute-start | bytes 6152 | tf_op jit(solution)/shard_map/ppermute | solution.py:18
  6.6 39.1 %copy-start.4 = (bf16[4,45,192]{2,0,1:T(4,128)(2,1)S(1)}, bf16[4,45,192]{2,0,1:T(4,128)(2,1)}, u32[]{:S(2)}) copy-start(bf16[4,45,192]{2,0,1:T(4,128)(2,1)} %param.7) | copy-start | bytes 207364
  6.6 33.0 %collective-permute-start.1 = (bf16[4,1,256]{2,0,1:T(4,128)(2,1)S(1)}, bf16[4,1,256]{2,0,1:T(4,128)(2,1)S(1)}, u32[]{:S(2)}, u32[]{:S(2)}) collective-permute-start(bf16[4,1,256]{2,0,1:T(4,128)(2,1)S(1)} %get-tuple-element.116), channel_id=1, source_target_pairs={{1,0},{2,1},{3,2},{4,3},{5,4},{6,5},{7,6},{8,7},{9,8},{10,9},{11,1... | collective-permute-start | bytes 6152 | tf_op jit(solution)/shard_map/ppermute | solution.py:20
  39.8 6.0 %collective-permute-start.2 = (bf16[1,47,256]{2,0,1:T(2,128)(2,1)S(1)}, bf16[1,47,256]{2,0,1:T(2,128)(2,1)S(1)}, u32[]{:S(2)}, u32[]{:S(2)}) collective-permute-start(bf16[1,47,256]{2,0,1:T(2,128)(2,1)S(1)} %get-tuple-element.100), channel_id=1, source_target_pairs={{0,32},{32,64},{64,96},{96,128},{128,160},{160,192},{192,224},{224... | collective-permute-start | bytes 72200 | tf_op jit(solution)/shard_map/ppermute | solution.py:18
  43.8 5.4 %collective-permute-start.3 = (bf16[1,47,256]{2,0,1:T(2,128)(2,1)S(1)}, bf16[1,47,256]{2,0,1:T(2,128)(2,1)S(1)}, u32[]{:S(2)}, u32[]{:S(2)}) collective-permute-start(bf16[1,47,256]{2,0,1:T(2,128)(2,1)S(1)} %get-tuple-element.101), channel_id=1, source_target_pairs={{32,0},{64,32},{96,64},{128,96},{160,128},{192,160},{224,192},{256... | collective-permute-start | bytes 72200 | tf_op jit(solution)/shard_map/ppermute | solution.py:20
  52.8 29.3 %collective-permute-start.4 = (bf16[4,1,256]{2,0,1:T(4,128)(2,1)S(1)}, bf16[4,1,256]{2,0,1:T(4,128)(2,1)S(1)}, u32[]{:S(2)}, u32[]{:S(2)}) collective-permute-start(bf16[4,1,256]{2,0,1:T(4,128)(2,1)S(1)} %get-tuple-element.114), channel_id=1, source_target_pairs={{0,1},{1,2},{2,3},{3,4},{4,5},{5,6},{6,7},{7,8},{8,9},{9,10},{10,1... | collective-permute-start | bytes 6152 | tf_op jit(solution)/shard_map/ppermute | solution.py:18
  74.5 8.3 %collective-permute-start.5 = (bf16[4,1,256]{2,0,1:T(4,128)(2,1)S(1)}, bf16[4,1,256]{2,0,1:T(4,128)(2,1)S(1)}, u32[]{:S(2)}, u32[]{:S(2)}) collective-permute-start(bf16[4,1,256]{2,0,1:T(4,128)(2,1)S(1)} %get-tuple-element.113), channel_id=1, source_target_pairs={{1,0},{2,1},{3,2},{4,3},{5,4},{6,5},{7,6},{8,7},{9,8},{10,9},{11,1... | collective-permute-start | bytes 6152 | tf_op jit(solution)/shard_map/ppermute | solution.py:20
  82.9 5.0 %collective-permute-start.6 = (bf16[1,47,256]{2,0,1:T(2,128)(2,1)S(1)}, bf16[1,47,256]{2,0,1:T(2,128)(2,1)S(1)}, u32[]{:S(2)}, u32[]{:S(2)}) collective-permute-start(bf16[1,47,256]{2,0,1:T(2,128)(2,1)S(1)} %get-tuple-element.98), channel_id=1, source_target_pairs={{0,32},{32,64},{64,96},{96,128},{128,160},{160,192},{192,224},{224... | collective-permute-start | bytes 72200 | tf_op jit(solution)/shard_map/ppermute | solution.py:18
  85.9 5.4 %collective-permute-start.7 = (bf16[1,47,256]{2,0,1:T(2,128)(2,1)S(1)}, bf16[1,47,256]{2,0,1:T(2,128)(2,1)S(1)}, u32[]{:S(2)}, u32[]{:S(2)}) collective-permute-start(bf16[1,47,256]{2,0,1:T(2,128)(2,1)S(1)} %get-tuple-element.99), channel_id=1, source_target_pairs={{32,0},{64,32},{96,64},{128,96},{160,128},{192,160},{224,192},{256... | collective-permute-start | bytes 72200 | tf_op jit(solution)/shard_map/ppermute | solution.py:20
  95.0 10.8 %collective-permute-start.8 = (bf16[4,1,256]{2,0,1:T(4,128)(2,1)S(1)}, bf16[4,1,256]{2,0,1:T(4,128)(2,1)S(1)}, u32[]{:S(2)}, u32[]{:S(2)}) collective-permute-start(bf16[4,1,256]{2,0,1:T(4,128)(2,1)S(1)} %get-tuple-element.109), channel_id=1, source_target_pairs={{0,1},{1,2},{2,3},{3,4},{4,5},{5,6},{6,7},{7,8},{8,9},{9,10},{10,1... | collective-permute-start | bytes 6152 | tf_op jit(solution)/shard_map/ppermute | solution.py:18
  97.7 8.8 %collective-permute-start.9 = (bf16[4,1,256]{2,0,1:T(4,128)(2,1)S(1)}, bf16[4,1,256]{2,0,1:T(4,128)(2,1)S(1)}, u32[]{:S(2)}, u32[]{:S(2)}) collective-permute-start(bf16[4,1,256]{2,0,1:T(4,128)(2,1)S(1)} %get-tuple-element.108), channel_id=1, source_target_pairs={{1,0},{2,1},{3,2},{4,3},{5,4},{6,5},{7,6},{8,7},{9,8},{10,9},{11,1... | collective-permute-start | bytes 6152 | tf_op jit(solution)/shard_map/ppermute | solution.py:20
  106.6 4.8 %collective-permute-start.10 = (bf16[1,47,256]{2,0,1:T(2,128)(2,1)S(1)}, bf16[1,47,256]{2,0,1:T(2,128)(2,1)S(1)}, u32[]{:S(2)}, u32[]{:S(2)}) collective-permute-start(bf16[1,47,256]{2,0,1:T(2,128)(2,1)S(1)} %get-tuple-element.96), channel_id=1, source_target_pairs={{0,32},{32,64},{64,96},{96,128},{128,160},{160,192},{192,224},{224... | collective-permute-start | bytes 72200 | tf_op jit(solution)/shard_map/ppermute | solution.py:18
  109.4 5.4 %collective-permute-start.11 = (bf16[1,47,256]{2,0,1:T(2,128)(2,1)S(1)}, bf16[1,47,256]{2,0,1:T(2,128)(2,1)S(1)}, u32[]{:S(2)}, u32[]{:S(2)}) collective-permute-start(bf16[1,47,256]{2,0,1:T(2,128)(2,1)S(1)} %get-tuple-element.97), channel_id=1, source_target_pairs={{32,0},{64,32},{96,64},{128,96},{160,128},{192,160},{224,192},{256... | collective-permute-start | bytes 72200 | tf_op jit(solution)/shard_map/ppermute | solution.py:20
  119.4 19.7 %all-to-all-start = ((bf16[32,2,720]{2,1,0:T(2,128)(2,1)}), bf16[32,2,720]{2,1,0:T(2,128)(2,1)S(1)}, u32[]{:S(2)}, u32[]{:S(2)}) async-start(bf16[32,2,720]{2,1,0:T(2,128)(2,1)} %reshape.151), calls=%async_computation | async-start | bytes 196608 | tf_op jit(solution)/shard_map/all_to_all | solution.py:89
  139.6 7.3 %slice-start = ((s8[4472832]{0:T(1024)(128)(4,1)}), s8[278528]{0:T(1024)(128)(4,1)S(1)}, s32[]{:S(2)}) async-start(s8[4472832]{0:T(1024)(128)(4,1)} %bitcast.189), calls=%async_computation.2 | async-start | bytes 557056
  153.9 40.3 %copy-start.1 = (bf16[9,64,64]{1,2,0:T(8,128)(2,1)S(1)}, bf16[9,64,64]{1,2,0:T(8,128)(2,1)}, u32[]{:S(2)}) copy-start(bf16[9,64,64]{1,2,0:T(8,128)(2,1)} %get-tuple-element.32) | copy-start | bytes 221188
  155.8 15.8 %all-to-all-start.1 = ((bf16[32,2,720]{2,1,0:T(2,128)(2,1)}), bf16[32,2,720]{2,1,0:T(2,128)(2,1)S(1)}, u32[]{:S(2)}, u32[]{:S(2)}) async-start(bf16[32,2,720]{2,1,0:T(2,128)(2,1)} %reshape.153), calls=%async_computation.1 | async-start | bytes 196608 | tf_op jit(solution)/shard_map/all_to_all | solution.py:119
  176.1 9.5 %collective-permute-start.12 = (bf16[4,1,256]{2,0,1:T(4,128)(2,1)S(1)}, bf16[4,1,256]{2,0,1:T(4,128)(2,1)S(1)}, u32[]{:S(2)}, u32[]{:S(2)}) collective-permute-start(bf16[4,1,256]{2,0,1:T(4,128)(2,1)S(1)} %get-tuple-element.106), channel_id=1, source_target_pairs={{0,1},{1,2},{2,3},{3,4},{4,5},{5,6},{6,7},{7,8},{8,9},{9,10},{10,1... | collective-permute-start | bytes 6152 | tf_op jit(solution)/shard_map/ppermute | solution.py:18
  178.8 7.6 %collective-permute-start.13 = (bf16[4,1,256]{2,0,1:T(4,128)(2,1)S(1)}, bf16[4,1,256]{2,0,1:T(4,128)(2,1)S(1)}, u32[]{:S(2)}, u32[]{:S(2)}) collective-permute-start(bf16[4,1,256]{2,0,1:T(4,128)(2,1)S(1)} %get-tuple-element.107), channel_id=1, source_target_pairs={{1,0},{2,1},{3,2},{4,3},{5,4},{6,5},{7,6},{8,7},{9,8},{10,9},{11,1... | collective-permute-start | bytes 6152 | tf_op jit(solution)/shard_map/ppermute | solution.py:20
  186.5 8.4 %collective-permute-start.14 = (bf16[1,47,256]{2,0,1:T(2,128)(2,1)S(1)}, bf16[1,47,256]{2,0,1:T(2,128)(2,1)S(1)}, u32[]{:S(2)}, u32[]{:S(2)}) collective-permute-start(bf16[1,47,256]{2,0,1:T(2,128)(2,1)S(1)} %get-tuple-element.94), channel_id=1, source_target_pairs={{0,32},{32,64},{64,96},{96,128},{128,160},{160,192},{192,224},{224... | collective-permute-start | bytes 72200 | tf_op jit(solution)/shard_map/ppermute | solution.py:18
  192.0 5.4 %collective-permute-start.15 = (bf16[1,47,256]{2,0,1:T(2,128)(2,1)S(1)}, bf16[1,47,256]{2,0,1:T(2,128)(2,1)S(1)}, u32[]{:S(2)}, u32[]{:S(2)}) collective-permute-start(bf16[1,47,256]{2,0,1:T(2,128)(2,1)S(1)} %get-tuple-element.95), channel_id=1, source_target_pairs={{32,0},{64,32},{96,64},{128,96},{160,128},{192,160},{224,192},{256... | collective-permute-start | bytes 72200 | tf_op jit(solution)/shard_map/ppermute | solution.py:20
  201.1 10.1 %collective-permute-start.16 = (bf16[4,1,256]{2,0,1:T(4,128)(2,1)S(1)}, bf16[4,1,256]{2,0,1:T(4,128)(2,1)S(1)}, u32[]{:S(2)}, u32[]{:S(2)}) collective-permute-start(bf16[4,1,256]{2,0,1:T(4,128)(2,1)S(1)} %get-tuple-element.105), channel_id=1, source_target_pairs={{0,1},{1,2},{2,3},{3,4},{4,5},{5,6},{6,7},{7,8},{8,9},{9,10},{10,1... | collective-permute-start | bytes 6152 | tf_op jit(solution)/shard_map/ppermute | solution.py:18
  203.0 8.8 %collective-permute-start.17 = (bf16[4,1,256]{2,0,1:T(4,128)(2,1)S(1)}, bf16[4,1,256]{2,0,1:T(4,128)(2,1)S(1)}, u32[]{:S(2)}, u32[]{:S(2)}) collective-permute-start(bf16[4,1,256]{2,0,1:T(4,128)(2,1)S(1)} %get-tuple-element.104), channel_id=1, source_target_pairs={{1,0},{2,1},{3,2},{4,3},{5,4},{6,5},{7,6},{8,7},{9,8},{10,9},{11,1... | collective-permute-start | bytes 6152 | tf_op jit(solution)/shard_map/ppermute | solution.py:20
  212.0 5.5 %collective-permute-start.18 = (bf16[1,47,256]{2,0,1:T(2,128)(2,1)S(1)}, bf16[1,47,256]{2,0,1:T(2,128)(2,1)S(1)}, u32[]{:S(2)}, u32[]{:S(2)}) collective-permute-start(bf16[1,47,256]{2,0,1:T(2,128)(2,1)S(1)} %get-tuple-element.92), channel_id=1, source_target_pairs={{0,32},{32,64},{64,96},{96,128},{128,160},{160,192},{192,224},{224... | collective-permute-start | bytes 72200 | tf_op jit(solution)/shard_map/ppermute | solution.py:18
  214.7 5.4 %collective-permute-start.19 = (bf16[1,47,256]{2,0,1:T(2,128)(2,1)S(1)}, bf16[1,47,256]{2,0,1:T(2,128)(2,1)S(1)}, u32[]{:S(2)}, u32[]{:S(2)}) collective-permute-start(bf16[1,47,256]{2,0,1:T(2,128)(2,1)S(1)} %get-tuple-element.93), channel_id=1, source_target_pairs={{32,0},{64,32},{96,64},{128,96},{160,128},{192,160},{224,192},{256... | collective-permute-start | bytes 72200 | tf_op jit(solution)/shard_map/ppermute | solution.py:20
  220.9 17.5 %copy-start = (f32[4,45,256]{2,0,1:T(4,128)S(1)}, f32[4,45,256]{2,0,1:T(4,128)}, u32[]{:S(2)}) copy-start(f32[4,45,256]{2,0,1:T(4,128)} %param.5) | copy-start | bytes 552964
  222.9 10.1 %collective-permute-start.20 = (bf16[4,1,256]{2,0,1:T(4,128)(2,1)S(1)}, bf16[4,1,256]{2,0,1:T(4,128)(2,1)S(1)}, u32[]{:S(2)}, u32[]{:S(2)}) collective-permute-start(bf16[4,1,256]{2,0,1:T(4,128)(2,1)S(1)} %get-tuple-element.103), channel_id=1, source_target_pairs={{0,1},{1,2},{2,3},{3,4},{4,5},{5,6},{6,7},{7,8},{8,9},{9,10},{10,1... | collective-permute-start | bytes 6152 | tf_op jit(solution)/shard_map/ppermute | solution.py:18
  224.9 8.8 %collective-permute-start.21 = (bf16[4,1,256]{2,0,1:T(4,128)(2,1)S(1)}, bf16[4,1,256]{2,0,1:T(4,128)(2,1)S(1)}, u32[]{:S(2)}, u32[]{:S(2)}) collective-permute-start(bf16[4,1,256]{2,0,1:T(4,128)(2,1)S(1)} %get-tuple-element.102), channel_id=1, source_target_pairs={{1,0},{2,1},{3,2},{4,3},{5,4},{6,5},{7,6},{8,7},{9,8},{10,9},{11,1... | collective-permute-start | bytes 6152 | tf_op jit(solution)/shard_map/ppermute | solution.py:20
  233.8 8.6 %collective-permute-start.22 = (bf16[1,47,256]{2,0,1:T(2,128)(2,1)S(1)}, bf16[1,47,256]{2,0,1:T(2,128)(2,1)S(1)}, u32[]{:S(2)}, u32[]{:S(2)}) collective-permute-start(bf16[1,47,256]{2,0,1:T(2,128)(2,1)S(1)} %get-tuple-element.90), channel_id=1, source_target_pairs={{0,32},{32,64},{64,96},{96,128},{128,160},{160,192},{192,224},{224... | collective-permute-start | bytes 72200 | tf_op jit(solution)/shard_map/ppermute | solution.py:18
  236.5 5.9 %collective-permute-start.23 = (bf16[1,47,256]{2,0,1:T(2,128)(2,1)S(1)}, bf16[1,47,256]{2,0,1:T(2,128)(2,1)S(1)}, u32[]{:S(2)}, u32[]{:S(2)}) collective-permute-start(bf16[1,47,256]{2,0,1:T(2,128)(2,1)S(1)} %get-tuple-element.91), channel_id=1, source_target_pairs={{32,0},{64,32},{96,64},{128,96},{160,128},{192,160},{224,192},{256... | collective-permute-start | bytes 72200 | tf_op jit(solution)/shard_map/ppermute | solution.py:20
  359.2 109.5 %copy-start.5 = (f32[16,4]{0,1:T(4,128)}, f32[16,4]{0,1:T(4,128)S(1)}, u32[]{:S(2)}) copy-start(f32[16,4]{0,1:T(4,128)S(1)} %get-tuple-element.28) | copy-start | bytes 772
  (2 other events, 8.8 us)
where the time goes:
time: 478 us; the launch traced here: 469 us
  blocking collectives  203 us (42%)
  starting transfers between devices  111 us (23%)
  other arithmetic  43.9 us (9%)
  waiting for transfers between devices  41.5 us (9%)
  local copies, waits for them, and re-layouts  35.2 us (7%)
  matrix products  24.3 us (5%)
  between operations  9.91 us (2%)
    psum x1, blocking collectives, per_device(): diag_coef, stored_coef = lax.psum((part_diag, part_stored), ('lat', 'lon'))  108 us
    psum x1, blocking collectives, per_device(): gram_matrix = lax.psum(part_gram, ('lat', 'lon'))  94.6 us
    ppermute x12, starting transfers between devices, with_halo(): lax.ppermute(head, axis, [((i + 1) % count, i) for i in range(ends)])  62.9 us
    ppermute x12, starting transfers between devices, with_halo(): lax.ppermute(tail, axis, [(i, (i + 1) % count) for i in range(ends)])  36 us
    neg x1, other arithmetic, spectral(): backward_table = jnp.concatenate([cosine.T, -sine_table.T], axis=0)  19.8 us
    neg x1, other arithmetic, spectral(): forward_table = jnp.concatenate([cosine, -sine_table], axis=1)  19.7 us
    ppermute x12, waiting for transfers between devices, with_halo(): lax.ppermute(head, axis, [((i + 1) % count, i) for i in range(ends)])  18.6 us
    all_to_all x1, waiting for transfers between devices, spectral(): lax.all_to_all(restored, 'lon', split_axis=1, concat_axis=2, tiled=True)  11.6 us
  transfers between devices with their start and end apart: 26, of which 12 were waited for; matrix products, arithmetic and copies ran while one was open for 10% of the time, Pallas kernels for 0%

commit v1 on v0

--- a/solution.py
+++ b/solution.py
@@ -1,3 +1,4 @@
+import functools
 import jax
 import jax.numpy as jnp
 from jax import lax
@@ -5,6 +6,15 @@
 
 highest = lax.Precision.HIGHEST
 triple = lax.Precision.HIGH
+
+
+def _report_task(frame_in, lane_axis):
+    piece_now = lax.all_gather(frame_in, axis_name=lane_axis)
+    now = jnp.sum(piece_now, axis=0)
+    return now
+
+
+treat_members_all = functools.partial(_report_task, lane_axis=("lat", "lon"))
 
 
 def with_halo(cells, sides, width, closed):
@@ -156,7 +166,7 @@
     residual = image_cells - jnp.einsum("xvc,vw->xwc", current, diag_coef, precision=highest)
     residual = residual - jnp.einsum("xsc,sw->xwc", stored, stored_coef, precision=highest)
     part_gram = jnp.einsum("xvc,xwc->vw", residual, residual, precision=highest) * weighting
-    gram_matrix = lax.psum(part_gram, ("lat", "lon"))
+    gram_matrix = treat_members_all(part_gram)
     norm_factor, inverse = upper_factor(gram_matrix)
     next_fields = jnp.einsum("xvc,vw->xwc", residual, inverse, precision=highest)
     return (

time: 478 us -> 1860 us (3.89)
  the two profiles are of different devices: /device:TPU:1 before, /device:TPU:8 now
where the time goes in v1:
time: 1860 us; the launch traced here: 1850 us
  blocking collectives  1570 us (84%)
  starting transfers between devices  126 us (7%)
  other arithmetic  44.5 us (2%)
  waiting for transfers between devices  37.2 us (2%)
  local copies, waits for them, and re-layouts  35.2 us (2%)
  matrix products  24.3 us (1%)
    all_gather x1, blocking collectives, _report_task(): piece_now = lax.all_gather(frame_in, axis_name=lane_axis)  1480 us
    psum x1, blocking collectives, per_device(): diag_coef, stored_coef = lax.psum((part_diag, part_stored), ('lat', 'lon'))  97.3 us
    ppermute x12, starting transfers between devices, with_halo(): lax.ppermute(head, axis, [((i + 1) % count, i) for i in range(ends)])  86.8 us
  transfers between devices with their start and end apart: 26, of which 12 were waited for; matrix products, arithmetic and copies ran while one was open for 3% of the time, Pallas kernels for 0%

profile of v1, /device:TPU:8, one launch (start us, length us, event | category | flops | bytes accessed | tf_op | source)
XLA Modules:
  0.0 1849.4 jit_solution(4466769761318264082)
XLA Ops:
  1.6 4.4 collective-permute-start
  6.0 11.5 collective-permute-start.1
  17.6 19.7 %sine_negate_fusion.1 = (f32[1440,721]{1,0:T(8,128)}, f32[1440,721]{1,0:T(8,128)}) fusion(), kind=kLoop, calls=%fused_computation.20 | loop fusion | flops 10382400 | bytes 8305920 | tf_op jit(solution)/shard_map/neg | solution.py:115
  38.4 1.9 collective-permute-start.2
  40.3 5.8 collective-permute-start.3
  51.4 1.9 collective-permute-start.4
  53.4 19.8 %sine_negate_fusion = (f32[721,1440]{1,0:T(8,128)}, f32[721,1440]{1,0:T(8,128)}) fusion(), kind=kLoop, calls=%fused_computation.12 | loop fusion | flops 10382400 | bytes 8305920 | tf_op jit(solution)/shard_map/neg | solution.py:116
  73.1 8.1 collective-permute-start.5
  82.6 1.9 collective-permute-start.6
  84.6 5.8 collective-permute-start.7
  95.7 1.9 collective-permute-start.8
  98.4 8.4 collective-permute-start.9
  110.1 5.8 collective-permute-start.11
  122.2 8.6 all-to-all-start
  130.9 12.4 all-to-all-done
  144.2 7.0 fusion.20
  151.2 5.2 fusion.32
  158.1 1.9 reshape.157
  160.0 3.8 all-to-all-start.1
  164.2 12.1 all-to-all-done.1
  180.9 2.8 collective-permute-start.12
  183.7 7.3 collective-permute-start.13
  192.4 1.9 collective-permute-start.14
  194.3 5.9 collective-permute-start.15
  207.4 8.4 collective-permute-start.17
  219.1 5.8 collective-permute-start.19
  231.3 8.4 collective-permute-start.21
  241.1 1.9 collective-permute-start.22
  243.1 5.8 collective-permute-start.23
  254.3 3.3 concatenate.83
  261.1 97.3 %all-reduce = (f32[16,4]{0,1:T(4,128)S(1)}, f32[4,4]{0,1:T(4,128)S(1)}) all-reduce(f32[16,4]{0,1:T(4,128)S(1)} %fusion.43, f32[4,4]{0,1:T(4,128)S(1)} %fusion.45), channel_id=1, replica_groups=mesh['lat'=16,'lon'=32] {'lat','lon'}, use_global_device_ids=true, to_apply=%region_1.2 | all-reduce | flops 80 | bytes 640 | tf_op jit(solution)/shard_map/psum | solution.py:165
  360.6 1475.4 %all-gather.1 = f32[512,4,4]{2,1,0:T(4,128)S(1)} all-gather(f32[1,4,4]{2,1,0:T(4,128)S(1)} %fusion.44), channel_id=2, replica_groups=mesh['lat'=16,'lon'=32] {'lat','lon'}, dimensions={0}, use_global_device_ids=true | all-gather | bytes 32832 | tf_op jit(solution)/shard_map/all_gather | solution.py:12
  (214 shorter events, 67.4 us)
Async XLA Ops:
  1.6 35.7 %copy-start.3 = (bf16[3,9,64,64]{3,2,1,0:T(8,128)(2,1)S(1)}, bf16[3,9,64,64]{3,2,1,0:T(8,128)(2,1)}, u32[]{:S(2)}) copy-start(bf16[3,9,64,64]{3,2,1,0:T(8,128)(2,1)} %param.8) | copy-start | bytes 663556
  1.6 36.6 %collective-permute-start = (bf16[4,1,256]{2,0,1:T(4,128)(2,1)S(1)}, bf16[4,1,256]{2,0,1:T(4,128)(2,1)S(1)}, u32[]{:S(2)}, u32[]{:S(2)}) collective-permute-start(bf16[4,1,256]{2,0,1:T(4,128)(2,1)S(1)} %get-tuple-element.115), channel_id=1, source_target_pairs={{0,1},{1,2},{2,3},{3,4},{4,5},{5,6},{6,7},{7,8},{8,9},{9,10},{10,1... | collective-permute-start | bytes 6152 | tf_op jit(solution)/shard_map/ppermute | solution.py:28
  6.0 40.0 %copy-start.4 = (bf16[4,45,192]{2,0,1:T(4,128)(2,1)S(1)}, bf16[4,45,192]{2,0,1:T(4,128)(2,1)}, u32[]{:S(2)}) copy-start(bf16[4,45,192]{2,0,1:T(4,128)(2,1)} %param.7) | copy-start | bytes 207364
  6.0 32.1 %collective-permute-start.1 = (bf16[4,1,256]{2,0,1:T(4,128)(2,1)S(1)}, bf16[4,1,256]{2,0,1:T(4,128)(2,1)S(1)}, u32[]{:S(2)}, u32[]{:S(2)}) collective-permute-start(bf16[4,1,256]{2,0,1:T(4,128)(2,1)S(1)} %get-tuple-element.116), channel_id=1, source_target_pairs={{1,0},{2,1},{3,2},{4,3},{5,4},{6,5},{7,6},{8,7},{9,8},{10,9},{11,1... | collective-permute-start | bytes 6152 | tf_op jit(solution)/shard_map/ppermute | solution.py:30
  38.4 7.8 collective-permute-start.2
  40.3 7.5 collective-permute-start.3
  51.4 29.8 %collective-permute-start.4 = (bf16[4,1,256]{2,0,1:T(4,128)(2,1)S(1)}, bf16[4,1,256]{2,0,1:T(4,128)(2,1)S(1)}, u32[]{:S(2)}, u32[]{:S(2)}) collective-permute-start(bf16[4,1,256]{2,0,1:T(4,128)(2,1)S(1)} %get-tuple-element.114), channel_id=1, source_target_pairs={{0,1},{1,2},{2,3},{3,4},{4,5},{5,6},{6,7},{7,8},{8,9},{9,10},{10,1... | collective-permute-start | bytes 6152 | tf_op jit(solution)/shard_map/ppermute | solution.py:28
  73.1 9.4 collective-permute-start.5
  82.6 7.7 collective-permute-start.6
  84.6 7.5 collective-permute-start.7
  95.7 11.1 collective-permute-start.8
  98.4 9.7 collective-permute-start.9
  108.2 7.8 collective-permute-start.10
  110.1 7.5 collective-permute-start.11
  122.2 21.1 %all-to-all-start = ((bf16[32,2,720]{2,1,0:T(2,128)(2,1)}), bf16[32,2,720]{2,1,0:T(2,128)(2,1)S(1)}, u32[]{:S(2)}, u32[]{:S(2)}) async-start(bf16[32,2,720]{2,1,0:T(2,128)(2,1)} %reshape.155), calls=%async_computation | async-start | bytes 196608 | tf_op jit(solution)/shard_map/all_to_all | solution.py:99
  143.9 7.3 slice-start
  158.1 42.2 %copy-start.1 = (bf16[9,64,64]{1,2,0:T(8,128)(2,1)S(1)}, bf16[9,64,64]{1,2,0:T(8,128)(2,1)}, u32[]{:S(2)}) copy-start(bf16[9,64,64]{1,2,0:T(8,128)(2,1)} %get-tuple-element.32) | copy-start | bytes 221188
  160.0 16.3 all-to-all-start.1
  180.9 10.1 collective-permute-start.12
  183.7 8.6 collective-permute-start.13
  192.4 8.7 collective-permute-start.14
  194.3 7.5 collective-permute-start.15
  205.5 10.3 collective-permute-start.16
  207.4 9.7 collective-permute-start.17
  217.2 8.5 collective-permute-start.18
  219.1 7.5 collective-permute-start.19
  227.4 21.4 %copy-start = (f32[4,45,256]{2,0,1:T(4,128)S(1)}, f32[4,45,256]{2,0,1:T(4,128)}, u32[]{:S(2)}) copy-start(f32[4,45,256]{2,0,1:T(4,128)} %param.5) | copy-start | bytes 552964
  229.4 10.3 collective-permute-start.20
  231.3 9.7 collective-permute-start.21
  241.1 11.6 collective-permute-start.22
  243.1 9.7 collective-permute-start.23
  358.3 1490.8 %copy-start.5 = (f32[16,4]{0,1:T(4,128)}, f32[16,4]{0,1:T(4,128)S(1)}, u32[]{:S(2)}) copy-start(f32[16,4]{0,1:T(4,128)S(1)} %get-tuple-element.28) | copy-start | bytes 772
  (2 other events, 8.8 us)
